TPU v7x, 256 devices: a whole 4x4x8 slice. The times are simulated.
256 devices in a mesh: src: 32 (over y, z), tm: 8 (over x, core).
Axes of the slice: x: 4, y: 4, z: 8, core: 2. Of those that a mesh axis runs over, the one named last changes fastest.
Arguments:
- green: bfloat16 [8, 4096, 128, 128], P('tm', 'src'), may hold values from -0.046875 to 0.046875
- block_rows: int32 [8, 4096], P('tm', 'src'), may hold values from 0 to 31
- block_cols: int32 [8, 4096], P('tm', 'src'), may hold values from 0 to 31
- block_live: int32 [8, 4096], P('tm', 'src'), may hold values from 0 to 1, as said below
- data: float32 [8, 4096, 128], P('tm', 'src'), may hold values from -6 to 6
- row_weight: float32 [8, 4096], P('tm', 'src'), may hold values from 0.3 to 9
- source_gain: float32 [131072], P('src'), may hold values from 0.2 to 3
Outputs:
- solution: float32 [131072, 128], P(('src', 'tm'))
- residual: float32 [8, 4096, 128], P('tm', 'src')
- misfit: float32 [2, 128], replicated
Inputs may be any that keep to these rules, and one draw needn't show every extreme that they name: `block_live`: within one device's 128 slots every slot is live with the same chance, a chance that differs from device to device; in some device all 128 slots are live.
All inputs are finite; a program needn't handle non-finite values.
Results may differ from a plain program's by a relative error of at most 0.0038.
Values may be sent and summed in bfloat16 or wider, within the bound.
A program may use at most 128 MiB of HBM per device.

v0:
```python
import jax
import jax.numpy as jnp
from jax import lax
from jax.sharding import PartitionSpec as P

ITERS = 2
HIGH = lax.Precision.HIGHEST
EPSILON = 1e-06


def shards(green, block_rows, block_cols, block_live, data, row_weight, source_gain):
    blocks = green[0]
    slot_count = blocks.shape[0]
    block_size = blocks.shape[1]
    datasets = data.shape[2]
    own_rows = data.shape[1]
    own_blocks = own_rows // block_size
    groups = lax.axis_size("src")
    windows = lax.axis_size("tm")
    window_blocks = own_blocks * groups
    sources = source_gain.shape[0]
    col_blocks = sources // block_size
    share_rows = sources // windows
    total_rows = own_rows * groups * windows
    live_slots = block_live[0].astype(jnp.float32)[:, None]
    row_hit = block_rows[0][:, None] == jnp.arange(window_blocks, dtype=jnp.int32)[None, :]
    col_hit = block_cols[0][:, None] == jnp.arange(col_blocks, dtype=jnp.int32)[None, :]
    gather_rows = row_hit.astype(jnp.bfloat16)
    gather_cols = col_hit.astype(jnp.bfloat16)
    spread_rows = jnp.transpose(row_hit.astype(jnp.float32) * live_slots)
    spread_cols = jnp.transpose(col_hit.astype(jnp.float32) * live_slots)
    weight = row_weight[0][:, None]
    tm_index = lax.axis_index("tm")
    gain_group = source_gain[:, None]

    def adjoint(residual):
        sent = (weight * residual).astype(jnp.bfloat16).reshape(own_blocks, block_size * datasets)
        gathered = lax.all_gather(sent, "src", axis=0, tiled=True)
        picked = jnp.dot(gather_rows, gathered, preferred_element_type=jnp.bfloat16)
        products = jnp.einsum(
            "kac,kar->kcr",
            blocks,
            picked.reshape(slot_count, block_size, datasets),
            preferred_element_type=jnp.float32,
        )
        products = products.reshape(slot_count, block_size * datasets)
        return jnp.dot(spread_cols, products, precision=HIGH).reshape(sources, datasets)

    def steepest_of(residual):
        summed = lax.psum(adjoint(residual), "tm")
        steepest = gain_group * summed
        gamma_now = lax.psum(jnp.sum(steepest * steepest, axis=0), "src")
        return (steepest, gamma_now)

    residual = weight * data[0]
    steepest, gamma_now = steepest_of(residual)
    direction = steepest
    solution = jnp.zeros((share_rows, datasets), jnp.float32)
    misfits = []
    for iteration in range(ITERS):
        forward_picked = jnp.dot(
            gather_cols,
            (gain_group * direction)
            .astype(jnp.bfloat16)
            .reshape(col_blocks, block_size * datasets),
            preferred_element_type=jnp.bfloat16,
        )
        forward_products = jnp.einsum(
            "kac,kcr->kar",
            blocks,
            forward_picked.reshape(slot_count, block_size, datasets),
            preferred_element_type=jnp.float32,
        )
        forward_products = forward_products.reshape(slot_count, block_size * datasets)
        forward_summed = lax.psum_scatter(
            jnp.dot(spread_rows, forward_products, precision=HIGH),
            "src",
            scatter_dimension=0,
            tiled=True,
        )
        image = weight * forward_summed.reshape(own_rows, datasets)
        image_norm = lax.psum(jnp.sum(image * image, axis=0), ("src", "tm"))
        step_size = gamma_now / (image_norm + EPSILON)
        solution = solution + step_size * lax.dynamic_slice_in_dim(
            direction, tm_index * share_rows, share_rows, 0
        )
        residual = residual - step_size * image
        misfits.append(lax.psum(jnp.sum(residual * residual, axis=0), ("src", "tm")) / total_rows)
        if iteration + 1 < ITERS:
            steepest, gamma_next = steepest_of(residual)
            direction = steepest + gamma_next / (gamma_now + EPSILON) * direction
            gamma_now = gamma_next
    return (solution, residual[None], jnp.stack(misfits))


def solution(mesh):
    placed = (
        P("tm", "src", None, None),
        P("tm", "src"),
        P("tm", "src"),
        P("tm", "src"),
        P("tm", "src", None),
        P("tm", "src"),
        P("src"),
    )
    return jax.shard_map(
        shards,
        mesh=mesh,
        in_specs=placed,
        out_specs=(P(("src", "tm"), None), P("tm", "src", None), P()),
        check_vma=False,
    )
```

profile of v0, /device:TPU:1, one launch (start us, length us, event | category | flops | bytes accessed | tf_op | source)
XLA Modules:
  0.0 1052.1 jit_solution(14238654614562010378)
XLA Ops:
  10.2 78.8 %all-gather.5.cloned.1.call-done = bf16[32,1,16384]{2,1,0:T(2,128)(2,1)} async-done(((bf16[1,1,16384]{2,1,0:T(2,128)(2,1)}), bf16[32,1,16384]{2,1,0:T(2,128)(2,1)}) %all-gather.5.cloned.1.call-update) | async-done | bytes 1048592 | tf_op jit(solution)/shard_map/all_gather | solution.py:38
  89.1 3.2 convolution_bitcast_fusion.1
  94.5 4.8 fusion.10
  99.2 9.3 copy.27
  108.6 10.7 %fusion.43 = f32[32,16384]{1,0:T(8,128)S(1)} fusion(f32[128,16384]{0,1:T(8,128)} %bitcast.97, f32[128]{0:T(128)S(1)} %convert_bitcast_fusion.2, s32[128]{0:T(128)S(1)} %bitcast.117), kind=kOutput, calls=%fused_computation.48 | convolution fusion | flops 805314560 | bytes 10486784 | tf_op jit(solution)/shard_map/dot_general | solution.py:47
  121.3 69.5 %all-reduce.8.cloned.1.call-done = f32[4096,128]{1,0:T(8,128)} async-done(((f32[4096,128]{1,0:T(8,128)}), f32[4096,128]{1,0:T(8,128)}) %all-reduce.8.cloned.1.call-update) | async-done | bytes 2097168 | tf_op jit(solution)/shard_map/psum | solution.py:50
  190.9 1.9 multiply_convert_fusion.1
  194.1 2.7 fusion.29
  196.8 7.3 fusion.13
  204.1 9.4 copy.30
  213.4 11.7 %fusion.39 = f32[32,16384]{1,0:T(8,128)} fusion(f32[128,16384]{0,1:T(8,128)} %bitcast.98, s32[128]{0:T(128)S(1)} %bitcast.122, f32[128]{0:T(128)S(1)} %convert_bitcast_fusion.2), kind=kOutput, calls=%fused_computation.44 | convolution fusion | flops 805314560 | bytes 10486784 | tf_op jit(solution)/shard_map/dot_general | solution.py:76
  226.4 61.0 %psum.57 = f32[128]{0:T(128)S(1)} all-reduce(f32[128]{0:T(128)S(1)} %multiply_reduce_fusion.1), channel_id=1, replica_groups=mesh['src'=32,'tm'=8] {'src'}, use_global_device_ids=true, to_apply=%region_2.0 | all-reduce | flops 128 | bytes 1024 | tf_op jit(solution)/shard_map/psum | solution.py:52
  287.4 89.4 %all-reduce.12.cloned.1.call-done = f32[32,16384]{1,0:T(8,128)} async-done(((f32[32,16384]{1,0:T(8,128)}), f32[32,16384]{1,0:T(8,128)}) %all-reduce.12.cloned.1.call-update) | async-done | bytes 2097168
  376.8 1.7 constant_dynamic-slice_fusion.1
  378.6 78.4 %psum.58 = f32[128]{0:T(128)S(1)} all-reduce(f32[128]{0:T(128)S(1)} %multiply_reduce_fusion.5), channel_id=1, replica_groups=mesh['src'=32,'tm'=8] {'src','tm'}, use_global_device_ids=true, to_apply=%region_5.0 | all-reduce | flops 128 | bytes 1024 | tf_op jit(solution)/shard_map/psum | solution.py:82
  457.0 2.4 convert_bitcast_fusion
  459.7 69.4 %all-gather.7.cloned.1.call-done = bf16[32,1,16384]{2,1,0:T(2,128)(2,1)} async-done(((bf16[1,1,16384]{2,1,0:T(2,128)(2,1)}), bf16[32,1,16384]{2,1,0:T(2,128)(2,1)}) %all-gather.7.cloned.1.call-update) | async-done | bytes 1048592 | tf_op jit(solution)/shard_map/all_gather | solution.py:38
  529.1 3.2 convolution_bitcast_fusion
  534.5 4.7 fusion.18
  539.2 9.4 copy.32
  548.6 11.7 %fusion.41 = f32[32,16384]{1,0:T(8,128)} fusion(f32[128,16384]{0,1:T(8,128)} %bitcast.99, f32[128]{0:T(128)S(1)} %convert_bitcast_fusion.2, s32[128]{0:T(128)S(1)} %bitcast.119), kind=kOutput, calls=%fused_computation.46 | convolution fusion | flops 805314560 | bytes 10486784 | tf_op jit(solution)/shard_map/dot_general | solution.py:47
  560.3 2.7 reshape.254
  563.0 70.0 %all-reduce.10.cloned.1.call-done = f32[4096,128]{1,0:T(8,128)} async-done(((f32[4096,128]{1,0:T(8,128)}), f32[4096,128]{1,0:T(8,128)}) %all-reduce.10.cloned.1.call-update) | async-done | bytes 2097168 | tf_op jit(solution)/shard_map/psum | solution.py:50
  633.1 1.9 multiply_reduce_fusion
  635.0 61.2 %psum.60 = f32[128]{0:T(128)S(1)} all-reduce(f32[128]{0:T(128)S(1)} %multiply_reduce_fusion), channel_id=1, replica_groups=mesh['src'=32,'tm'=8] {'src'}, use_global_device_ids=true, to_apply=%region_8.0 | all-reduce | flops 128 | bytes 1024 | tf_op jit(solution)/shard_map/psum | solution.py:52
  696.2 3.3 multiply_convert_fusion
  703.2 7.3 fusion.21
  710.4 9.4 copy.35
  719.8 11.7 %fusion.37 = f32[32,16384]{1,0:T(8,128)} fusion(f32[128,16384]{0,1:T(8,128)} %bitcast.96, s32[128]{0:T(128)S(1)} %bitcast.124, f32[128]{0:T(128)S(1)} %convert_bitcast_fusion.2), kind=kOutput, calls=%fused_computation.42 | convolution fusion | flops 805314560 | bytes 10486784 | tf_op jit(solution)/shard_map/dot_general | solution.py:76
  731.6 157.0 %all-reduce.14.cloned.1.call-done = f32[32,16384]{1,0:T(8,128)} async-done(((f32[32,16384]{1,0:T(8,128)}), f32[32,16384]{1,0:T(8,128)}) %all-reduce.14.cloned.1.call-update) | async-done | bytes 2097168
  890.4 78.4 %psum.61 = f32[128]{0:T(128)S(1)} all-reduce(f32[128]{0:T(128)S(1)} %multiply_reduce_fusion.4), channel_id=1, replica_groups=mesh['src'=32,'tm'=8] {'src','tm'}, use_global_device_ids=true, to_apply=%region_11.0 | all-reduce | flops 128 | bytes 1024 | tf_op jit(solution)/shard_map/psum | solution.py:82
  968.9 73.1 %all-reduce.2 = (f32[128]{0:T(128)S(1)}, f32[128]{0:T(128)S(1)}) all-reduce(f32[128]{0:T(128)S(1)} %get-tuple-element.4, f32[128]{0:T(128)S(1)} %get-tuple-element.3), channel_id=1, replica_groups=mesh['src'=32,'tm'=8] {'src','tm'}, use_global_device_ids=true, to_apply=%region_15.0 | all-reduce | flops 256 | bytes 2048 | tf_op jit(solution)/shard_map/psum | solution.py:88
  (55 shorter events, 21.0 us)
Async XLA Ops:
  7.2 81.9 %all-gather.5.cloned.1.call-start = ((), (), s32[]{:S(2)}) async-start(), calls=%async_computation.2 | async-start | bytes 2162688 | tf_op jit(solution)/shard_map/all_gather | solution.py:38
  9.5 181.3 %all-reduce.8.cloned.1.call-start = ((), (), s32[]{:S(2)}) async-start(), calls=%async_computation | async-start | bytes 4194304 | tf_op jit(solution)/shard_map/psum | solution.py:50
  92.3 2.2 copy-start
  99.2 9.3 copy-start.7
  119.3 71.6 %copy-start.5 = (f32[4096]{0:T(1024)S(1)}, f32[4096]{0:T(1024)}, u32[]{:S(2)}) copy-start(f32[4096]{0:T(1024)} %param.13) | copy-start | bytes 49156
  120.8 256.0 %all-reduce.12.cloned.1.call-start = ((), (), s32[]{:S(2)}) async-start(), calls=%async_computation.4 | async-start | bytes 4194304
  194.1 2.7 copy-start.1
  204.1 9.4 copy-start.8
  213.4 11.8 %copy-start.9 = (u32[256]{0:T(256)S(1)}, u32[256]{0:T(256)}, u32[]{:S(2)}) copy-start(u32[256]{0:T(256)} %constant.28) | copy-start | bytes 3076
  225.1 153.4 %copy-start.6 = (f32[1,128]{1,0:T(1,128)S(1)}, f32[1,128]{1,0:T(1,128)}, u32[]{:S(2)}) copy-start(f32[1,128]{1,0:T(1,128)} %param.12) | copy-start | bytes 1540
  225.2 303.9 %all-gather.7.cloned.1.call-start = ((), (), s32[]{:S(2)}) async-start(), calls=%async_computation.3 | async-start | bytes 2162688 | tf_op jit(solution)/shard_map/all_gather | solution.py:38
  459.5 173.6 %all-reduce.10.cloned.1.call-start = ((), (), s32[]{:S(2)}) async-start(), calls=%async_computation.1 | async-start | bytes 4194304 | tf_op jit(solution)/shard_map/psum | solution.py:50
  532.3 2.2 copy-start.2
  563.0 325.6 %all-reduce.14.cloned.1.call-start = ((), (), s32[]{:S(2)}) async-start(), calls=%async_computation.5 | async-start | bytes 4194304
  701.0 2.2 copy-start.3
  719.8 249.0 %copy-start.4 = (f32[1,128,128]{2,1,0:T(8,128)S(1)}, f32[1,128,128]{2,1,0:T(8,128)}, u32[]{:S(2)}) copy-start(f32[1,128,128]{2,1,0:T(8,128)} %param.11) | copy-start | bytes 196612
Sparse Core Ops, SparseCore 0:
  11.2 77.8 all-gather.4
  120.9 69.8 all-reduce.7
  225.3 151.4 all-reduce.11
  459.6 69.4 all-gather.6
  563.1 69.8 all-reduce.9
  731.7 156.8 all-reduce.13
where the time goes:
time: 1060 us; the launch traced here: 1050 us
  waiting for transfers between devices  534 us (50%)
  blocking collectives  352 us (33%)
  matrix products  80.3 us (8%)
  local copies, waits for them, and re-layouts  54.4 us (5%)
  other arithmetic  15.6 us (1%)
  between operations  14.5 us (1%)
    unnamed x8, waiting for transfers between devices  247 us
    psum x2, blocking collectives, shards(): image_norm = lax.psum(jnp.sum(image * image, axis=0), ('src', 'tm'))  157 us
    all_gather x2, waiting for transfers between devices, adjoint(): gathered = lax.all_gather(sent, 'src', axis=0, tiled=True)  148 us
    psum x2, waiting for transfers between devices, steepest_of(): summed = lax.psum(adjoint(residual), 'tm')  140 us
    psum x2, blocking collectives, steepest_of(): gamma_now = lax.psum(jnp.sum(steepest * steepest, axis=0), 'src')  122 us
    psum x1, blocking collectives, shards(): lax.psum(jnp.sum(residual * residual, axis=0), ('src', 'tm')) / total_rows  73.1 us
    dot_general x2, matrix products, shards(): jnp.dot(spread_rows, forward_products, precision=HIGH)  23.4 us
    dot_general x2, matrix products, adjoint(): jnp.dot(spread_cols, products, precision=HIGH).reshape(sources, datasets)  22.4 us
  transfers between devices with their start and end apart: 6, of which 6 were waited for; matrix products, arithmetic and copies ran while one was open for 0% of the time, Pallas kernels for 0%

commit v1 on v0

--- a/solution.py
+++ b/solution.py
@@ -85,7 +85,10 @@
             direction, tm_index * share_rows, share_rows, 0
         )
         residual = residual - step_size * image
-        misfits.append(lax.psum(jnp.sum(residual * residual, axis=0), ("src", "tm")) / total_rows)
+        misfits.append(
+            jnp.sum(lax.all_gather(jnp.sum(residual * residual, axis=0), ("src", "tm")), axis=0)
+            / total_rows
+        )
         if iteration + 1 < ITERS:
             steepest, gamma_next = steepest_of(residual)
             direction = steepest + gamma_next / (gamma_now + EPSILON) * direction

time: 1060 us -> 1090 us (1.028)
  blocking collectives: 352 us -> 385 us
    all_gather x0 -> x2, blocking collectives: none -> 106 us  [shards(): lax.all_gather(jnp.sum(residual * residual, axis=0), ('src', 'tm'))]
    psum x1 -> x0, blocking collectives: 73.1 us -> none  [shards(): lax.psum(jnp.sum(residual * residual, axis=0), ('src', 'tm')) / total_rows]
where the time goes in v1:
time: 1090 us
  waiting for transfers between devices  534 us (49%)
  blocking collectives  385 us (35%)
  matrix products  80.3 us (7%)
  local copies, waits for them, and re-layouts  54.4 us (5%)
  other arithmetic  16.2 us (1%)
  between operations  14.5 us (1%)
    unnamed x8, waiting for transfers between devices  247 us
    psum x2, blocking collectives, shards(): image_norm = lax.psum(jnp.sum(image * image, axis=0), ('src', 'tm'))  157 us
    all_gather x2, waiting for transfers between devices, adjoint(): gathered = lax.all_gather(sent, 'src', axis=0, tiled=True)  148 us
    psum x2, waiting for transfers between devices, steepest_of(): summed = lax.psum(adjoint(residual), 'tm')  140 us
    psum x2, blocking collectives, steepest_of(): gamma_now = lax.psum(jnp.sum(steepest * steepest, axis=0), 'src')  122 us
    all_gather x2, blocking collectives, shards(): lax.all_gather(jnp.sum(residual * residual, axis=0), ('src', 'tm'))  106 us
    dot_general x2, matrix products, shards(): jnp.dot(spread_rows, forward_products, precision=HIGH)  23.4 us
    dot_general x2, matrix products, adjoint(): jnp.dot(spread_cols, products, precision=HIGH).reshape(sources, datasets)  22.4 us
  transfers between devices with their start and end apart: 6, of which 6 were waited for; matrix products, arithmetic and copies ran while one was open for 0% of the time, Pallas kernels for 0%

profile of v1, /device:TPU:1, one launch (start us, length us, event | category | flops | bytes accessed | tf_op | source)
XLA Modules:
  0.0 1086.1 jit_solution(1725961482852934098)
XLA Ops:
  10.2 78.8 %all-gather.9.cloned.1.call-done = bf16[32,1,16384]{2,1,0:T(2,128)(2,1)} async-done(((bf16[1,1,16384]{2,1,0:T(2,128)(2,1)}), bf16[32,1,16384]{2,1,0:T(2,128)(2,1)}) %all-gather.9.cloned.1.call-update) | async-done | bytes 1048592 | tf_op jit(solution)/shard_map/all_gather | solution.py:38
  89.1 3.2 convolution_bitcast_fusion.1
  94.5 4.8 fusion.10
  99.2 9.3 copy.27
  108.6 10.7 fusion.43
  121.3 69.5 %all-reduce.7.cloned.1.call-done = f32[4096,128]{1,0:T(8,128)} async-done(((f32[4096,128]{1,0:T(8,128)}), f32[4096,128]{1,0:T(8,128)}) %all-reduce.7.cloned.1.call-update) | async-done | bytes 2097168 | tf_op jit(solution)/shard_map/psum | solution.py:50
  190.9 1.9 multiply_convert_fusion.1
  194.1 2.7 fusion.29
  196.8 7.3 fusion.13
  204.1 9.4 copy.30
  213.4 11.7 %fusion.39 = f32[32,16384]{1,0:T(8,128)} fusion(f32[128,16384]{0,1:T(8,128)} %bitcast.100, s32[128]{0:T(128)S(1)} %bitcast.124, f32[128]{0:T(128)S(1)} %convert_bitcast_fusion.2), kind=kOutput, calls=%fused_computation.44 | convolution fusion | flops 805314560 | bytes 10486784 | tf_op jit(solution)/shard_map/dot_general | solution.py:76
  226.4 61.0 %psum.43 = f32[128]{0:T(128)S(1)} all-reduce(f32[128]{0:T(128)S(1)} %multiply_reduce_fusion.1), channel_id=1, replica_groups=mesh['src'=32,'tm'=8] {'src'}, use_global_device_ids=true, to_apply=%region_2.0 | all-reduce | flops 128 | bytes 1024 | tf_op jit(solution)/shard_map/psum | solution.py:52
  287.4 89.4 %all-reduce.11.cloned.1.call-done = f32[32,16384]{1,0:T(8,128)} async-done(((f32[32,16384]{1,0:T(8,128)}), f32[32,16384]{1,0:T(8,128)}) %all-reduce.11.cloned.1.call-update) | async-done | bytes 2097168
  378.6 78.4 %psum.44 = f32[128]{0:T(128)S(1)} all-reduce(f32[128]{0:T(128)S(1)} %multiply_reduce_fusion.5), channel_id=1, replica_groups=mesh['src'=32,'tm'=8] {'src','tm'}, use_global_device_ids=true, to_apply=%region_5.0 | all-reduce | flops 128 | bytes 1024 | tf_op jit(solution)/shard_map/psum | solution.py:82
  457.0 2.4 convert_bitcast_fusion
  459.7 69.4 %all-gather.11.cloned.1.call-done = bf16[32,1,16384]{2,1,0:T(2,128)(2,1)} async-done(((bf16[1,1,16384]{2,1,0:T(2,128)(2,1)}), bf16[32,1,16384]{2,1,0:T(2,128)(2,1)}) %all-gather.11.cloned.1.call-update) | async-done | bytes 1048592 | tf_op jit(solution)/shard_map/all_gather | solution.py:38
  529.1 3.2 convolution_bitcast_fusion
  534.5 4.7 fusion.18
  539.2 9.4 copy.32
  548.6 11.7 %fusion.41 = f32[32,16384]{1,0:T(8,128)} fusion(f32[128,16384]{0,1:T(8,128)} %bitcast.101, f32[128]{0:T(128)S(1)} %convert_bitcast_fusion.2, s32[128]{0:T(128)S(1)} %bitcast.121), kind=kOutput, calls=%fused_computation.46 | convolution fusion | flops 805314560 | bytes 10486784 | tf_op jit(solution)/shard_map/dot_general | solution.py:47
  560.3 2.7 reshape.272
  563.0 70.1 %all-reduce.9.cloned.1.call-done = f32[4096,128]{1,0:T(8,128)} async-done(((f32[4096,128]{1,0:T(8,128)}), f32[4096,128]{1,0:T(8,128)}) %all-reduce.9.cloned.1.call-update) | async-done | bytes 2097168 | tf_op jit(solution)/shard_map/psum | solution.py:50
  633.1 1.9 multiply_reduce_fusion
  635.1 61.2 %psum.46 = f32[128]{0:T(128)S(1)} all-reduce(f32[128]{0:T(128)S(1)} %multiply_reduce_fusion), channel_id=1, replica_groups=mesh['src'=32,'tm'=8] {'src'}, use_global_device_ids=true, to_apply=%region_8.0 | all-reduce | flops 128 | bytes 1024 | tf_op jit(solution)/shard_map/psum | solution.py:52
  696.3 3.3 multiply_convert_fusion
  703.2 7.3 fusion.21
  710.5 9.4 copy.35
  719.9 11.7 %fusion.37 = f32[32,16384]{1,0:T(8,128)} fusion(f32[128,16384]{0,1:T(8,128)} %bitcast.98, s32[128]{0:T(128)S(1)} %bitcast.126, f32[128]{0:T(128)S(1)} %convert_bitcast_fusion.2), kind=kOutput, calls=%fused_computation.42 | convolution fusion | flops 805314560 | bytes 10486784 | tf_op jit(solution)/shard_map/dot_general | solution.py:76
  731.6 157.0 %all-reduce.13.cloned.1.call-done = f32[32,16384]{1,0:T(8,128)} async-done(((f32[32,16384]{1,0:T(8,128)}), f32[32,16384]{1,0:T(8,128)}) %all-reduce.13.cloned.1.call-update) | async-done | bytes 2097168
  890.5 78.4 %psum.47 = f32[128]{0:T(128)S(1)} all-reduce(f32[128]{0:T(128)S(1)} %multiply_reduce_fusion.4), channel_id=1, replica_groups=mesh['src'=32,'tm'=8] {'src','tm'}, use_global_device_ids=true, to_apply=%region_11.0 | all-reduce | flops 128 | bytes 1024 | tf_op jit(solution)/shard_map/psum | solution.py:82
  969.0 53.3 %all-gather.5 = f32[256,1,128]{2,1,0:T(1,128)S(1)} all-gather(f32[1,1,128]{2,1,0:T(1,128)S(1)} %bitcast.128), channel_id=3, replica_groups=mesh['src'=32,'tm'=8] {'src','tm'}, dimensions={0}, use_global_device_ids=true | all-gather | bytes 131584 | tf_op jit(solution)/shard_map/all_gather | solution.py:89
  1022.6 53.2 %all-gather.4 = f32[256,1,128]{2,1,0:T(1,128)S(1)} all-gather(f32[1,1,128]{2,1,0:T(1,128)S(1)} %bitcast.127), channel_id=2, replica_groups=mesh['src'=32,'tm'=8] {'src','tm'}, dimensions={0}, use_global_device_ids=true | all-gather | bytes 131584 | tf_op jit(solution)/shard_map/all_gather | solution.py:89
  (59 shorter events, 23.3 us)
Async XLA Ops:
  7.2 81.9 %all-gather.9.cloned.1.call-start = ((), (), s32[]{:S(2)}) async-start(), calls=%async_computation.2 | async-start | bytes 2162688 | tf_op jit(solution)/shard_map/all_gather | solution.py:38
  9.5 181.3 %all-reduce.7.cloned.1.call-start = ((), (), s32[]{:S(2)}) async-start(), calls=%async_computation | async-start | bytes 4194304 | tf_op jit(solution)/shard_map/psum | solution.py:50
  92.3 2.2 copy-start
  99.2 9.3 copy-start.7
  119.3 71.6 %copy-start.5 = (f32[4096]{0:T(1024)S(1)}, f32[4096]{0:T(1024)}, u32[]{:S(2)}) copy-start(f32[4096]{0:T(1024)} %param.13) | copy-start | bytes 49156
  120.8 256.0 %all-reduce.11.cloned.1.call-start = ((), (), s32[]{:S(2)}) async-start(), calls=%async_computation.4 | async-start | bytes 4194304
  194.1 2.7 copy-start.1
  204.1 9.4 copy-start.8
  213.4 11.8 %copy-start.9 = (u32[256]{0:T(256)S(1)}, u32[256]{0:T(256)}, u32[]{:S(2)}) copy-start(u32[256]{0:T(256)} %constant.28) | copy-start | bytes 3076
  225.1 153.4 %copy-start.6 = (f32[1,128]{1,0:T(1,128)S(1)}, f32[1,128]{1,0:T(1,128)}, u32[]{:S(2)}) copy-start(f32[1,128]{1,0:T(1,128)} %param.12) | copy-start | bytes 1540
  225.2 303.9 %all-gather.11.cloned.1.call-start = ((), (), s32[]{:S(2)}) async-start(), calls=%async_computation.3 | async-start | bytes 2162688 | tf_op jit(solution)/shard_map/all_gather | solution.py:38
  459.5 173.7 %all-reduce.9.cloned.1.call-start = ((), (), s32[]{:S(2)}) async-start(), calls=%async_computation.1 | async-start | bytes 4194304 | tf_op jit(solution)/shard_map/psum | solution.py:50
  532.3 2.2 copy-start.2
  563.0 325.7 %all-reduce.13.cloned.1.call-start = ((), (), s32[]{:S(2)}) async-start(), calls=%async_computation.5 | async-start | bytes 4194304
  701.1 2.2 copy-start.3
  719.9 249.0 %copy-start.4 = (f32[1,128,128]{2,1,0:T(8,128)S(1)}, f32[1,128,128]{2,1,0:T(8,128)}, u32[]{:S(2)}) copy-start(f32[1,128,128]{2,1,0:T(8,128)} %param.11) | copy-start | bytes 196612
Sparse Core Ops, SparseCore 0:
  11.2 77.8 all-gather.8
  120.9 69.8 all-reduce.6
  225.3 151.4 all-reduce.10
  459.6 69.4 all-gather.10
  563.1 69.9 all-reduce.8
  731.8 156.8 all-reduce.12
